TPU v7x, 256 devices: a whole 4x4x8 slice. The times are simulated.
256 devices in a mesh: group: 16 (over y_lo, x, core), narrow: 16 (over y_hi, z).
Axes of the slice: x: 4, y: 4 (y_hi: 2, y_lo: 2; y = y_hi * 2 + y_lo), z: 8, core: 2. Of those that a mesh axis runs over, the one named last changes fastest.
Arguments:
- patches: bfloat16 [4096, 3675], P(('group', 'narrow')), may hold values from -8 to 8
- counts: int32 [4096], P(('group', 'narrow')), may hold values from 1 to 49
- weights: float32 [49], replicated, may hold values from 0.3 to 3
- probes: float32 [4096, 16], P(('group', 'narrow')), may hold values from -6 to 6
- plan: int32 [4, 16], replicated, may hold values from 0 to 15, as said below
Outputs:
- product: float32 [4096, 16], P(('group', 'narrow'))
Inputs may be any that keep to these rules, and one draw needn't show every extreme that they name: Each row pairs the 16 blocks: plan[m, plan[m, b]] = b and plan[m, b] != b.
All inputs are finite; a program needn't handle non-finite values.
Results may differ from a plain program's by a relative error of at most 0.008.
Values may be sent and summed in bfloat16 or wider, within the bound.
A program may use at most 64 MiB of HBM per device.

v0:
```python
import jax
import jax.numpy as jnp
from jax import lax
from jax.sharding import PartitionSpec as P

P_SIZE = 49
PV = 75
NPROBE = 16
MEET = 4


def kernel_tile(rows_x, rows_n, cols_x, cols_n):
    inner = lax.dot_general(
        rows_x, cols_x, (((1,), (1,)), ((), ())), preferred_element_type=jnp.float32
    )
    return jnp.exp((2.0 * inner - rows_n[:, None] - cols_n[None, :]) / (2.0 * PV)).astype(
        jnp.bfloat16
    )


def squared(values):
    as_float = values.astype(jnp.float32)
    return jnp.sum(as_float * as_float, axis=1)


def shards(patches, counts, weights, probes, plan):
    images = patches.shape[0]
    span = images * P_SIZE
    local_x = patches.reshape(span, PV)
    valid = (jnp.arange(P_SIZE, dtype=jnp.int32)[None, :] < counts[:, None]).astype(jnp.float32)
    alpha = weights[None, :] * valid / counts[:, None].astype(jnp.float32)
    local_u = (alpha[:, :, None] * probes[:, None, :]).astype(jnp.bfloat16).reshape(span, NPROBE)
    local_a = alpha.reshape(span)
    block_x, block_u, block_a = (
        lax.all_gather(local_x, "narrow", axis=0, tiled=True),
        lax.all_gather(local_u, "narrow", axis=0, tiled=True),
        lax.all_gather(local_a.astype(jnp.bfloat16), "narrow", axis=0, tiled=True).astype(
            local_a.dtype
        ),
    )
    far_x, far_u, far_a = (
        lax.all_gather(local_x, "group", axis=0, tiled=True),
        lax.all_gather(local_u, "group", axis=0, tiled=True),
        lax.all_gather(local_a.astype(jnp.bfloat16), "group", axis=0, tiled=True).astype(
            local_a.dtype
        ),
    )
    subs = lax.axis_size("narrow")
    group_id = lax.axis_index("group")
    far_n = squared(far_x)
    rows_x = block_x.reshape(subs, span, PV)
    rows_n = squared(block_x).reshape(subs, span)
    rows_a = block_a.reshape(subs, span)
    direct = jnp.zeros((subs, span, NPROBE), jnp.float32)
    for meeting in range(MEET):
        partner = lax.dynamic_index_in_dim(plan[meeting], group_id, 0, keepdims=False)
        start = partner * span
        partner_cols_x = lax.dynamic_slice_in_dim(far_x, start, span, 0)
        partner_cols_n = lax.dynamic_slice_in_dim(far_n, start, span, 0)
        partner_cols_u = lax.dynamic_slice_in_dim(far_u, start, span, 0)
        cols_a = lax.dynamic_slice_in_dim(far_a, start, span, 0)
        partner, cols_x, cols_n, cols_u, cols_a = (
            partner,
            partner_cols_x,
            partner_cols_n,
            partner_cols_u,
            cols_a,
        )

        def one_sub(operands):
            energy = kernel_tile(operands[0], operands[1], cols_x, cols_n)
            return jnp.dot(energy, cols_u, preferred_element_type=jnp.float32)

        direct = direct + lax.map(one_sub, (rows_x, rows_n))
    terms = (direct * rows_a[:, :, None]).reshape(subs * images, P_SIZE, NPROBE).sum(axis=1)
    product = lax.psum_scatter(terms, "narrow", scatter_dimension=0, tiled=True)
    return product


def solution(mesh):
    return jax.shard_map(
        shards,
        mesh=mesh,
        in_specs=(
            P(("group", "narrow"), None),
            P(("group", "narrow")),
            P(),
            P(("group", "narrow"), None),
            P(),
        ),
        out_specs=P(("group", "narrow"), None),
        check_vma=False,
    )
```

profile of v0, /device:TPU:1, one launch (start us, length us, event | category | flops | bytes accessed | tf_op | source)
XLA Modules:
  0.0 486.3 jit_solution(3247677797807378056)
XLA Ops:
  20.5 22.5 %all-gather.2 = bf16[16,784,16]{1,2,0:T(8,128)(2,1)S(1)} all-gather(bf16[1,784,16]{1,2,0:T(8,128)(2,1)S(1)} %fusion.56), channel_id=1, replica_groups=mesh['group'=16,'narrow'=16] {'group'}, dimensions={0}, use_global_device_ids=true | all-gather | bytes 426496 | tf_op jit(solution)/shard_map/all_gather | solution.py:43
  45.1 66.1 %all-reduce = bf16[12544]{0:T(1024)(128)(2,1)S(1)} all-reduce(bf16[12544]{0:T(1024)(128)(2,1)S(1)} %dynamic-update-slice), channel_id=1, replica_groups=mesh['group'=16,'narrow'=16] {'narrow'}, use_global_device_ids=true, to_apply=%add | all-reduce | flops 12544 | bytes 50176
  113.9 3.4 copy.39
  117.4 3.8 reshape.106
  122.3 14.8 %all-gather.6.cloned.1.call-done = bf16[16,784,75]{1,2,0:T(8,128)(2,1)} async-done(((bf16[1,784,75]{1,2,0:T(8,128)(2,1)}), bf16[16,784,75]{1,2,0:T(8,128)(2,1)}) %all-gather.6.cloned.1.call-update) | async-done | bytes 1881616 | tf_op jit(solution)/shard_map/all_gather | solution.py:35
  137.1 4.8 copy.42
  142.5 32.5 %while.41 = (s32[]{:T(128)}, f32[16,784,16]{1,2,0:T(8,128)S(1)}, bf16[16,784,75]{2,1,0:T(8,128)(2,1)}, bf16[784,75]{1,0:T(8,128)(2,1)S(1)}, f32[16,784]{1,0:T(8,...) while((s32[]{:T(128)}, f32[16,784,16]{1,2,0:T(8,128)S(1)}, ...), condition=%wide.region_5.6_spmd, body=%wide.region_4.5_spmd.sunk | while | flops 114940672 | bytes 503001 | solution.py:74
  142.5 2.0 fusion.94
  146.6 2.0 fusion.94
  150.7 2.0 fusion.94
  154.7 2.0 fusion.94
  158.8 2.0 fusion.94
  175.3 32.3 %while.40 = (s32[]{:T(128)}, f32[16,784,16]{1,2,0:T(8,128)S(1)}, bf16[16,784,75]{2,1,0:T(8,128)(2,1)}, bf16[784,75]{1,0:T(8,128)(2,1)S(1)}, f32[16,784]{1,0:T(8,...) while((s32[]{:T(128)}, f32[16,784,16]{1,2,0:T(8,128)S(1)}, ...), condition=%wide.region_3.4_spmd, body=%wide.region_2.3_spmd.sunk | while | flops 114940672 | bytes 503001 | solution.py:74
  207.9 32.5 %while.42 = (s32[]{:T(128)}, f32[16,784,16]{1,2,0:T(8,128)S(1)}, bf16[16,784,75]{2,1,0:T(8,128)(2,1)}, bf16[784,75]{1,0:T(8,128)(2,1)S(1)}, f32[16,784]{1,0:T(8,...) while((s32[]{:T(128)}, f32[16,784,16]{1,2,0:T(8,128)S(1)}, ...), condition=%wide.region_7.8_spmd, body=%wide.region_6.7_spmd.sunk | while | flops 114940672 | bytes 503001 | solution.py:74
  241.6 42.4 %while.43 = (s32[]{:T(128)}, f32[16,784,16]{1,2,0:T(8,128)}, bf16[16,784,75]{2,1,0:T(8,128)(2,1)}, bf16[784,75]{1,0:T(8,128)(2,1)S(1)}, f32[16,784]{1,0:T(8,128)...) while((s32[]{:T(128)}, f32[16,784,16]{1,2,0:T(8,128)}, ...), condition=%wide.region_9.10_spmd, body=%wide.region_8.9_spmd.sunk | while | flops 114940672 | bytes 414393 | solution.py:74
  241.6 2.6 fusion.102
  244.3 2.6 fusion.102
  246.9 2.6 fusion.102
  249.6 2.6 fusion.102
  252.2 2.6 fusion.102
  254.9 2.6 fusion.102
  257.5 2.6 fusion.102
  260.2 2.6 fusion.102
  262.9 2.6 fusion.102
  265.5 2.6 fusion.102
  268.1 2.6 fusion.102
  270.8 2.6 fusion.102
  273.5 2.6 fusion.102
  276.1 2.6 fusion.102
  278.8 2.6 fusion.102
  281.4 2.6 fusion.102
  288.8 191.1 %reduce-scatter.4.cloned.1.call-done = f32[16,16]{1,0:T(8,128)} async-done(((f32[256,16]{1,0:T(8,128)}), f32[16,16]{1,0:T(8,128)}) %reduce-scatter.4.cloned.1.call-update) | async-done | bytes 1040 | tf_op jit(solution)/shard_map/reduce_scatter | solution.py:76
  (161 shorter events, 106.1 us)
Async XLA Ops:
  6.5 37.0 %copy-start.1 = (u32[256]{0:T(256)S(1)}, u32[256]{0:T(256)}, u32[]{:S(2)}) copy-start(u32[256]{0:T(256)} %constant.94) | copy-start | bytes 3076
  6.5 107.4 %all-gather.8.cloned.1.call-start = ((), (), s32[]{:S(2)}) async-start(), calls=%async_computation.2 | async-start | bytes 2437120 | tf_op jit(solution)/shard_map/all_gather | solution.py:42
  8.5 128.5 %all-gather.6.cloned.1.call-start = ((), (), s32[]{:S(2)}) async-start(), calls=%async_computation.1 | async-start | bytes 2437120 | tf_op jit(solution)/shard_map/all_gather | solution.py:35
  9.3 470.6 %reduce-scatter.4.cloned.1.call-start = ((), (), s32[]{:S(2)}) async-start(), calls=%async_computation.3 | async-start | bytes 139264 | tf_op jit(solution)/shard_map/reduce_scatter | solution.py:76
  137.0 4.8 copy-start
Sparse Core Ops, SparseCore 0:
  9.2 41.9 all-gather.7
  53.8 83.1 all-gather.5
  288.9 190.8 reduce-scatter.3
where the time goes:
time: 493 us; the launch traced here: 486 us
  waiting for transfers between devices  207 us (42%)
  matrix products  137 us (28%)
  blocking collectives  88.6 us (18%)
  local copies, waits for them, and re-layouts  26.7 us (5%)
  between operations  21.3 us (4%)
  other arithmetic  5.77 us (1%)
    reduce_scatter x1, waiting for transfers between devices, shards(): product = lax.psum_scatter(terms, 'narrow', scatter_dimension=0, tiled=True)  191 us
    dot_general x64, matrix products, one_sub(): return jnp.dot(energy, cols_u, preferred_element_type=jnp.float32)  137 us
    unnamed x1, blocking collectives  66.1 us
    all_gather x1, blocking collectives, shards(): lax.all_gather(local_u, 'group', axis=0, tiled=True)  22.5 us
    all_gather x1, waiting for transfers between devices, shards(): lax.all_gather(local_x, 'narrow', axis=0, tiled=True)  14.8 us
  transfers between devices with their start and end apart: 3, of which 2 were waited for; matrix products, arithmetic and copies ran while one was open for 3% of the time, Pallas kernels for 0%

commit v1 on v0

v1 whole, which is shorter than its diff:
```python
import functools

import jax
import jax.numpy as jnp
from jax import lax
from jax.experimental import pallas as pl
from jax.experimental.pallas import tpu as pltpu
from jax.sharding import PartitionSpec as P

P_SIZE = 49
PV = 75
NPROBE = 16
MEET = 4
IMGS = 16
GROUPS = 16
STEPS = 8
UNITS = 16
TILE = STEPS * UNITS
TILES = 7
DEPTH = 80
UROW = TILES * DEPTH
ROWS = UROW + 2 * NPROBE
SUBS = 10
LANES = 72
BLOCK = 2
RLIST = 32
FAR = -1.0e30
SCALE = 1.4426950408889634 / PV
MESH = pl.DeviceIdType.MESH
F32 = jnp.float32
BF16 = jnp.bfloat16
HALVES = ((0, 304), (304, 288))
VMEM = pl.BlockSpec(memory_space=pltpu.VMEM)
SMEM = pl.BlockSpec(memory_space=pltpu.SMEM)
ANY = pl.BlockSpec(memory_space=pl.ANY)


def two_parts(value):
    high = value.astype(BF16)
    return high, (value - high.astype(F32)).astype(BF16)


def pack_kernel(counts, weights, x_ref, probes_ref, item_ref, owner_ref):
    lane = lax.broadcasted_iota(jnp.int32, (1, TILES * TILE), 1)
    unit = lax.div(lane, TILE) * UNITS + lax.rem(lane, UNITS)
    step = lax.rem(lax.div(lane, UNITS), STEPS)
    whole = lax.broadcasted_iota(jnp.int32, (1, 128), 1)
    image, first, size = jnp.zeros_like(lane), jnp.zeros_like(lane), jnp.zeros_like(lane)
    owner = jnp.full_like(whole, -1)
    start = jnp.int32(0)
    for i in range(IMGS):
        count = counts[i]
        end = start + lax.div(count + (STEPS - 1), STEPS)
        inside = (unit >= start) & (unit < end)
        image = jnp.where(inside, i, image)
        first = jnp.where(inside, start, first)
        size = jnp.where(inside, count, size)
        owner = jnp.where((whole >= start) & (whole < end), i, owner)
        start = end
    patch = (unit - first) * STEPS + step
    valid = patch < size
    source = jnp.where(valid, image * P_SIZE + patch, -1)
    weight = jnp.ones(lane.shape, F32)
    for p in range(P_SIZE):
        weight = jnp.where(patch == p, weights[p], weight)
    alpha = weight / jnp.maximum(size, 1).astype(F32)
    rows = lax.broadcasted_iota(jnp.int32, (IMGS * P_SIZE, TILES * TILE), 0)
    pick = jnp.where(rows == source, 1.0, 0.0).astype(BF16)
    packed = lax.dot_general(
        x_ref[...], pick, (((0,), (0,)), ((), ())), preferred_element_type=F32
    )
    norm = jnp.sum(packed * packed, axis=0, keepdims=True)
    level = jnp.where(valid, PV * jnp.log(alpha) - 0.5 * norm, FAR)
    high = level.astype(BF16).astype(F32)
    low = level - high
    low = jnp.where(valid, low, 0.0)
    one = jnp.ones_like(level)
    full = jnp.concatenate([packed, high, low, one, one, jnp.zeros_like(one)], axis=0).astype(BF16)
    for t in range(TILES):
        item_ref[t * DEPTH : (t + 1) * DEPTH, :] = full[:, t * TILE : (t + 1) * TILE]
    tag = lax.broadcasted_iota(jnp.int32, (IMGS, 128), 0)
    mine = jnp.where(tag == owner, 1.0, 0.0).astype(BF16)
    owner_ref[...] = mine
    tiles = lax.div(start + (UNITS - 1), UNITS).astype(F32)
    lanes = lax.broadcasted_iota(jnp.int32, (NPROBE, 128), 1)
    for at, part in zip((UROW, UROW + NPROBE), two_parts(probes_ref[...])):
        spread = lax.dot_general(part, mine, (((0,), (0,)), ((), ())), preferred_element_type=F32)
        item_ref[at : at + NPROBE, :] = jnp.where(lanes >= 120, tiles, spread).astype(BF16)


def pack(x, counts, weights, probes):
    return pl.pallas_call(
        pack_kernel,
        out_shape=(
            jax.ShapeDtypeStruct((ROWS, 128), BF16),
            jax.ShapeDtypeStruct((IMGS, 128), BF16),
        ),
        in_specs=[SMEM, SMEM, VMEM, VMEM],
        out_specs=(VMEM, VMEM),
        name="pack",
    )(counts, weights, x, probes)


def places():
    g, n = lax.axis_index("group"), lax.axis_index("narrow")
    return g, n


def ring(n, by):
    return lax.div(n, 8) * 8 + lax.rem(lax.rem(n, 8) + by + 8, 8)


def along(g, by):
    return lax.div(g, 8) * 8 + lax.rem(lax.rem(g, 8) + 2 * by + 8, 8)


def flip(i):
    return lax.rem(i + 8, 16)


def sibling(g):
    return g + 1 - 2 * lax.rem(g, 2)


def gather_kernel(item, far, near, send_sem, recv_sem):
    g, n = places()
    up, down = ring(n, 1), ring(n, -1)
    right, left = along(g, 1), along(g, -1)
    over, twin = flip(g), sibling(g)
    peers = [(over, n), (right, n), (left, n), (twin, n), (g, up), (g, down), (over, flip(n))]
    barrier = pltpu.get_barrier_semaphore()
    for peer in peers:
        pl.semaphore_signal(barrier, inc=1, device_id=peer, device_id_type=MESH)
    pl.semaphore_wait(barrier, len(peers))

    def copy(which, half, src, dst, peer):
        at, size = HALVES[half]
        return pltpu.make_async_remote_copy(
            src_ref=src.at[pl.ds(at, size)],
            dst_ref=dst.at[pl.ds(at, size)],
            send_sem=send_sem.at[which, half],
            recv_sem=recv_sem.at[which, half],
            device_id=peer,
            device_id_type=MESH,
        )

    def across(which, owner, peer):
        return lambda half: copy(which, half, far.at[owner], far.at[owner], peer)

    def first(which, dst, peer):
        return lambda half: copy(which, half, item, dst, peer)

    plan = {
        "y": first(0, far.at[g], (over, n)),
        "right": first(1, far.at[g], (right, n)),
        "left": first(2, far.at[g], (left, n)),
        "up": first(3, near.at[1], (g, up)),
        "twin": first(4, far.at[g], (twin, n)),
        "yz": lambda half: copy(5, half, far.at[over], near.at[0], (over, flip(n))),
        "yright": across(6, over, (right, n)),
        "yleft": across(7, over, (left, n)),
        "right2": across(8, left, (right, n)),
        "yleft2": across(9, flip(right), (left, n)),
        "up2": lambda half: copy(10, half, near.at[1], near.at[2], (g, up)),
        "up3": lambda half: copy(11, half, near.at[2], near.at[3], (g, up)),
        "up4": lambda half: copy(12, half, near.at[3], near.at[4], (g, up)),
        "down": lambda half: copy(13, half, near.at[0], near.at[5], (g, down)),
        "down2": lambda half: copy(14, half, near.at[5], near.at[6], (g, down)),
        "down3": lambda half: copy(15, half, near.at[6], near.at[7], (g, down)),
        "down4": lambda half: copy(16, half, near.at[7], near.at[8], (g, down)),
        "ty": across(17, over, (twin, n)),
        "tleft": across(18, left, (twin, n)),
        "tright": across(19, right, (twin, n)),
        "tyleft": across(20, flip(left), (twin, n)),
        "tyright": across(21, flip(right), (twin, n)),
        "tfar": across(22, along(g, 2), (twin, n)),
        "tyfar": across(23, flip(along(g, 2)), (twin, n)),
    }
    for half in range(2):
        for name in ("y", "up", "right", "left", "twin"):
            plan[name](half).start()
    arrivals = [
        [("y", ("yz", "yright", "yleft", "ty")), ("up", ("up2",)), ("right", ("right2", "tleft")), ("left", ("tright",))],
        [("yz", ("down",)), ("up2", ("up3",)), ("yleft", ("yleft2", "tyright")), ("yright", ("tyleft",))],
        [("up3", ("up4",)), ("down", ("down2",)), ("right2", ("tfar",)), ("yleft2", ("tyfar",))],
        [("down2", ("down3",)), ("down3", ("down4",)), ("up4", ()), ("down4", ())],
    ]
    for wave in arrivals:
        for half in range(2):
            for name, onward in wave:
                plan[name](half).wait_recv()
                for other in onward:
                    plan[other](half).start()
    for half in range(2):
        for name in ("twin", "ty", "tleft", "tright", "tyleft", "tyright", "tfar", "tyfar"):
            plan[name](half).wait_recv()
    for half in range(2):
        for name in plan:
            plan[name](half).wait_send()


def gather(item):
    return pl.pallas_call(
        gather_kernel,
        out_shape=(
            jax.ShapeDtypeStruct((GROUPS, ROWS, 128), BF16),
            jax.ShapeDtypeStruct((9, ROWS, 128), BF16),
        ),
        in_specs=[ANY],
        out_specs=(ANY, ANY),
        scratch_shapes=[pltpu.SemaphoreType.DMA((24, 2)), pltpu.SemaphoreType.DMA((24, 2))],
        compiler_params=pltpu.CompilerParams(collective_id=0, has_side_effects=True),
        name="gather",
    )(item)


def tile_count(block):
    lanes = lax.broadcasted_iota(jnp.int32, block.shape, 1)
    return jnp.max(jnp.where(lanes >= 120, block.astype(F32), 0.0)).astype(jnp.int32)


def meet_kernel(
    plan, item, near, far, near_out, far_out,
    subs, parts, cols, col_u, rows, row_u, q_list, p_list, p_whole, q_whole, sems,
):
    g = lax.axis_index("group")
    partner = [plan[m, g] for m in range(MEET)]
    order = [item, near.at[0], near.at[1], near.at[2], near.at[3], near.at[5], near.at[6], near.at[7], near.at[4], near.at[8]]
    loads = [pltpu.make_async_copy(src, subs.at[r], sems.at[r]) for r, src in enumerate(order)]
    loads += [
        pltpu.make_async_copy(far.at[partner[m]], parts.at[m], sems.at[SUBS + m]) for m in range(MEET)
    ]
    for load in loads:
        load.start()
    q_list[...] = jnp.zeros_like(q_list)
    p_list[...] = jnp.zeros_like(p_list)
    p_whole[...] = jnp.zeros_like(p_whole)
    q_whole[...] = jnp.zeros_like(q_whole)
    far_out[...] = jnp.zeros_like(far_out)
    depth = lax.broadcasted_iota(jnp.int32, (DEPTH, TILE), 0)
    empty_cols = jnp.where(depth == PV, FAR, 0.0).astype(BF16)
    lane = lax.broadcasted_iota(jnp.int32, (TILE, DEPTH), 1)
    empty_rows = jnp.where(lane == PV + 2, FAR, 0.0).astype(BF16)
    a = lax.broadcasted_iota(jnp.int32, (DEPTH, DEPTH), 0)
    b = lax.broadcasted_iota(jnp.int32, (DEPTH, DEPTH), 1)
    moved = jnp.where(a < PV, a, jnp.where(a < PV + 2, a + 2, jnp.where(a < PV + 4, a - 2, a)))
    swap = jnp.where(moved == b, 1.0, 0.0).astype(BF16)
    for load in loads:
        load.wait()

    def spread_units(block):
        return jnp.transpose(block.astype(F32), (1, 0)).astype(BF16)

    at = jnp.int32(0)
    col_at, col_tiles, edges = [], [], [at]
    for r in range(SUBS):
        tiles = tile_count(subs[r, UROW : UROW + NPROBE, :])
        units = spread_units(subs[r, UROW:ROWS, :])
        for t in range(TILES):

            @pl.when(t < tiles)
            def _():
                cols[at + t] = subs[r, t * DEPTH : (t + 1) * DEPTH, :]
                col_u[at + t] = jnp.concatenate([units[t * UNITS : (t + 1) * UNITS]] * STEPS, axis=0)

        col_at.append(at)
        col_tiles.append(tiles)
        at = at + tiles
        if r in (1, 7, 9):
            cols[at] = empty_cols
            col_u[at] = jnp.zeros((TILE, 2 * NPROBE), BF16)
            at = lax.div(at + 1, 2) * 2
            edges.append(lax.div(at, 2))

    row_tiles = [tile_count(parts[m, UROW : UROW + NPROBE, :]) for m in range(MEET)]
    later = [partner[m] > g for m in range(MEET)]
    row_at = [jnp.int32(0)] * MEET
    at = jnp.int32(0)
    middle = at
    for side in range(2):
        for m in range(MEET):
            here = later[m] if side == 0 else jnp.logical_not(later[m])
            row_at[m] = jnp.where(here, at, row_at[m])
            at = at + jnp.where(here, row_tiles[m], 0)
        for extra in range(BLOCK - 1):
            rows[at + extra] = empty_rows
            row_u[at + extra] = jnp.zeros((UNITS, 2 * NPROBE), BF16)
        at = lax.div(at + BLOCK - 1, BLOCK) * BLOCK
        if side == 0:
            middle = lax.div(at, BLOCK)
    last = lax.div(at, BLOCK)
    for m in range(MEET):
        units = spread_units(parts[m, UROW:ROWS, :])
        for t in range(TILES):

            @pl.when(t < row_tiles[m])
            def _():
                turned = lax.dot_general(
                    parts[m, t * DEPTH : (t + 1) * DEPTH, :], swap,
                    (((0,), (0,)), ((), ())), preferred_element_type=F32,
                )
                rows[row_at[m] + t] = turned.astype(BF16)
                row_u[row_at[m] + t] = units[t * UNITS : (t + 1) * UNITS]

    def job(first_pair, last_pair, first_block, last_block):
        def pair_body(pair, carry):
            right = jnp.concatenate([cols[2 * pair], cols[2 * pair + 1]], axis=1)
            right_u = jnp.concatenate([col_u[2 * pair], col_u[2 * pair + 1]], axis=0)

            def block_body(block, total):
                left = rows[pl.ds(block * BLOCK, BLOCK)].reshape(BLOCK * TILE, DEPTH)
                left_u = row_u[pl.ds(block * BLOCK, BLOCK)].reshape(BLOCK * UNITS, 2 * NPROBE)
                inner = jnp.dot(left, right, preferred_element_type=F32)
                energy = jnp.exp2(inner * SCALE)
                sums = energy.reshape(BLOCK, STEPS, UNITS, 2 * TILE).sum(axis=1)
                sums = sums.reshape(BLOCK * UNITS, 2 * TILE).astype(BF16)
                q = jnp.dot(sums, right_u, preferred_element_type=F32)
                q_list[pl.ds(block * BLOCK, BLOCK)] += q.reshape(BLOCK, UNITS, 2 * NPROBE)
                return total + lax.dot_general(
                    left_u, sums, (((0,), (0,)), ((), ())), preferred_element_type=F32
                )

            total = lax.fori_loop(
                first_block, last_block, block_body, jnp.zeros((2 * NPROBE, 2 * TILE), F32)
            )
            p_list[2 * pair] += total[:, :TILE]
            p_list[2 * pair + 1] += total[:, TILE:]
            return carry

        lax.fori_loop(first_pair, last_pair, pair_body, 0)

    job(edges[0], edges[1], 0, middle)
    job(edges[1], edges[2], 0, last)
    job(edges[2], edges[3], middle, last)

    for r in range(SUBS):
        for t in range(TILES):

            @pl.when(t < col_tiles[r])
            def _():
                both = p_list[col_at[r] + t]
                high, low = two_parts(both[:NPROBE] + both[NPROBE:])
                p_whole[2 * r * NPROBE : (2 * r + 1) * NPROBE, t * TILE : (t + 1) * TILE] = high
                p_whole[(2 * r + 1) * NPROBE : (2 * r + 2) * NPROBE, t * TILE : (t + 1) * TILE] = low

    a = lax.broadcasted_iota(jnp.int32, (TILES * TILE, 128), 0)
    b = lax.broadcasted_iota(jnp.int32, (TILES * TILE, 128), 1)
    gather_units = jnp.where(lax.div(a, TILE) * UNITS + lax.rem(a, UNITS) == b, 1.0, 0.0).astype(BF16)
    units = jnp.dot(p_whole[...], gather_units, preferred_element_type=F32)
    for r in range(SUBS):
        near_out[r] = (
            units[2 * r * NPROBE : (2 * r + 1) * NPROBE]
            + units[(2 * r + 1) * NPROBE : (2 * r + 2) * NPROBE]
        )
    for m in range(MEET):
        for t in range(TILES):

            @pl.when(t < row_tiles[m])
            def _():
                q_whole[m, t * UNITS : (t + 1) * UNITS, : 2 * NPROBE] = q_list[row_at[m] + t]

        turned = jnp.transpose(q_whole[m], (1, 0))
        far_out[partner[m]] += turned[:NPROBE] + turned[NPROBE : 2 * NPROBE]


def meet(plan, item, near, far):
    return pl.pallas_call(
        meet_kernel,
        out_shape=(
            jax.ShapeDtypeStruct((SUBS, NPROBE, 128), F32),
            jax.ShapeDtypeStruct((GROUPS, NPROBE, 128), F32),
        ),
        in_specs=[SMEM, ANY, ANY, ANY],
        out_specs=(VMEM, VMEM),
        scratch_shapes=[
            pltpu.VMEM((SUBS, ROWS, 128), BF16),
            pltpu.VMEM((MEET, ROWS, 128), BF16),
            pltpu.VMEM((LANES, DEPTH, TILE), BF16),
            pltpu.VMEM((LANES, TILE, 2 * NPROBE), BF16),
            pltpu.VMEM((RLIST, TILE, DEPTH), BF16),
            pltpu.VMEM((RLIST, UNITS, 2 * NPROBE), BF16),
            pltpu.VMEM((RLIST, UNITS, 2 * NPROBE), F32),
            pltpu.VMEM((LANES, 2 * NPROBE, TILE), F32),
            pltpu.VMEM((SUBS * 2 * NPROBE, TILES * TILE), BF16),
            pltpu.VMEM((MEET, 128, 128), F32),
            pltpu.SemaphoreType.DMA((SUBS + MEET,)),
        ],
        name="meet",
    )(plan, item, near, far)


def home_kernel(near_part, far_part, owner, out, from_near, from_far, near_send, near_recv, far_send, far_recv):
    g, n = places()
    barrier = pltpu.get_barrier_semaphore()
    for k in range(1, 16):
        pl.semaphore_signal(barrier, inc=1, device_id=(g, lax.rem(n + k, 16)), device_id_type=MESH)
        pl.semaphore_signal(barrier, inc=1, device_id=(lax.rem(g + k, 16), n), device_id_type=MESH)
    pl.semaphore_wait(barrier, 30)
    across = flip(n)
    targets = [across, ring(n, -1), ring(n, -2), ring(n, -3), ring(across, 1), ring(across, 2), ring(across, 3), ring(n, -4), ring(across, 4)]
    copies = []
    for j, target in enumerate(targets):
        copies.append(
            pltpu.make_async_remote_copy(
                src_ref=near_part.at[j + 1], dst_ref=from_near.at[j],
                send_sem=near_send.at[j], recv_sem=near_recv.at[j],
                device_id=(g, target), device_id_type=MESH,
            )
        )
    for k in range(1, 16):
        target = lax.rem(g + k, 16)
        copies.append(
            pltpu.make_async_remote_copy(
                src_ref=far_part.at[target], dst_ref=from_far.at[k - 1],
                send_sem=far_send.at[k - 1], recv_sem=far_recv.at[k - 1],
                device_id=(target, n), device_id_type=MESH,
            )
        )
    for one in copies:
        one.start()
    for one in copies:
        one.wait_recv()
    total = near_part[0]
    for j in range(9):
        total = total + from_near[j]
    for k in range(15):
        total = total + from_far[k]
    result = jnp.zeros((IMGS, NPROBE), F32)
    rest = total
    for part in range(3):
        piece = rest.astype(BF16)
        rest = rest - piece.astype(F32)
        result = result + lax.dot_general(
            owner[...], piece, (((1,), (1,)), ((), ())), preferred_element_type=F32
        )
    out[...] = result
    for one in copies:
        one.wait_send()


def home(near_part, far_part, owner):
    return pl.pallas_call(
        home_kernel,
        out_shape=jax.ShapeDtypeStruct((IMGS, NPROBE), F32),
        in_specs=[VMEM, VMEM, VMEM],
        out_specs=VMEM,
        scratch_shapes=[
            pltpu.VMEM((9, NPROBE, 128), F32),
            pltpu.VMEM((15, NPROBE, 128), F32),
            pltpu.SemaphoreType.DMA((9,)),
            pltpu.SemaphoreType.DMA((9,)),
            pltpu.SemaphoreType.DMA((15,)),
            pltpu.SemaphoreType.DMA((15,)),
        ],
        compiler_params=pltpu.CompilerParams(collective_id=1, has_side_effects=True),
        name="home",
    )(near_part, far_part, owner)


def shards(patches, counts, weights, probes, plan):
    item, owner = pack(patches.reshape(IMGS * P_SIZE, PV), counts, weights, probes)
    far, near = gather(item)
    near_part, far_part = meet(plan, item, near, far)
    return home(near_part, far_part, owner)


def solution(mesh):
    return jax.shard_map(
        shards,
        mesh=mesh,
        in_specs=(
            P(("group", "narrow"), None),
            P(("group", "narrow")),
            P(),
            P(("group", "narrow"), None),
            P(),
        ),
        out_specs=P(("group", "narrow"), None),
        check_vma=False,
    )
```

time: 493 us -> 124 us (0.25); the launches traced: 486 us -> 124 us
  waiting for transfers between devices: 207 us -> 0 us
  matrix products: 137 us -> 0 us
  Pallas kernels: 0 us -> 121 us
  blocking collectives: 88.6 us -> 0 us
  local copies, waits for them, and re-layouts: 26.7 us -> 3.09 us
  between operations: 21.3 us -> 0.03 us
  other arithmetic: 5.77 us -> 0 us
    reduce_scatter x1 -> x0, waiting for transfers between devices: 191 us -> none  [shards(): product = lax.psum_scatter(terms, 'narrow', scatter_dimension=0, tiled=True)]
    dot_general x64 -> x0, matrix products: 137 us -> none  [one_sub(): return jnp.dot(energy, cols_u, preferred_element_type=jnp.float32)]
    pallas_call x0 -> x4, Pallas kernels: none -> 121 us  [the longest x1 53.2 us: meet(): pl.pallas_call(meet_kernel, out_shape=(jax.ShapeDtypeStruct((SUBS, NPROBE...]
    unnamed x1 -> x0, blocking collectives: 66.1 us -> none
    all_gather x1 -> x0, blocking collectives: 22.5 us -> none  [shards(): lax.all_gather(local_u, 'group', axis=0, tiled=True)]
    all_gather x2 -> x0, waiting for transfers between devices: 14.8 us -> none  [the longest x1 14.8 us: shards(): lax.all_gather(local_x, 'narrow', axis=0, tiled=True)]
    unnamed x13 -> x1, local copies, waits for them, and re-layouts: 8.67 us -> 1.3 us
    while x5 -> x0, local copies, waits for them, and re-layouts: 5.6 us -> none  [shards(): direct = direct + lax.map(one_sub, (rows_x, rows_n))]
  transfers between devices with their start and end apart: 3 -> 0, of which waited for: 2 -> 0; matrix products, arithmetic and copies ran while one was open for 3% -> 0% of each run, Pallas kernels for 0% -> 0%
where the time goes in v1:
time: 124 us
  Pallas kernels  121 us (98%)
  local copies, waits for them, and re-layouts  3.09 us (2%)
    pallas_call x1, Pallas kernels, meet(): pl.pallas_call(meet_kernel, out_shape=(jax.ShapeDtypeStruct((SUBS, NPROBE...  53.2 us
    pallas_call x1, Pallas kernels, gather(): pl.pallas_call(gather_kernel, out_shape=(jax.ShapeDtypeStruct((GROUPS, RO...  36.9 us
    pallas_call x1, Pallas kernels, home(): pl.pallas_call(home_kernel, out_shape=jax.ShapeDtypeStruct((IMGS, NPROBE)...  28.4 us

profile of v1, /device:TPU:1, one launch (start us, length us, event | category | flops | bytes accessed | tf_op | source)
XLA Modules:
  0.0 123.9 jit_solution(2030806670807133088)
XLA Ops:
  0.0 1.8 %reshape.3.x_ref = bf16[784,75]{1,0:T(8,128)(2,1)} reshape(bf16[16,3675]{1,0:T(8,128)(2,1)} %param.5) | data formatting | bytes 235200 | tf_op jit(solution)/shard_map/reshape | solution.py:461
  1.8 2.3 %pack.1 = (bf16[592,128]{1,0:T(8,128)(2,1)}, bf16[16,128]{1,0:T(8,128)(2,1)}) custom-call(s32[16]{0:T(128)} %counts.1, f32[49]{0:T(128)} %weights.1, bf16[784,75]{1,0:T(8,128)(2,1)} %reshape.3.x_ref, f32[16,16]{1,0:T(8,128)} %probes_ref.1), custom_call_target="tpu_custom_call" | custom-call | tf_op jit(solution)/shard_map/pack/pallas_call | solution.py:92
  4.1 36.9 %gather.1 = (bf16[16,592,128]{2,1,0:T(8,128)(2,1)}, bf16[9,592,128]{2,1,0:T(8,128)(2,1)}) custom-call(bf16[592,128]{1,0:T(8,128)(2,1)} %get-tuple-element.11.item), custom_call_target="tpu_custom_call" | custom-call | tf_op jit(solution)/shard_map/gather/pallas_call | solution.py:203
  41.0 53.2 %meet.1 = (f32[10,16,128]{2,1,0:T(8,128)}, f32[16,16,128]{2,1,0:T(8,128)}) custom-call(s32[4,16]{1,0:T(4,128)} %plan.1, bf16[592,128]{1,0:T(8,128)(2,1)} %get-tuple-element.11.item, bf16[9,592,128]{2,1,0:T(8,128)(2,1)} %get-tuple-element.12.near, bf16[16,592,128]{2,1,0:T(8,128)(2,1)} %get-tuple-element.13.far), custom_call_target="tpu_custom_call" | custom-call | tf_op jit(solution)/shard_map/meet/pallas_call | solution.py:367
  94.2 28.4 %home.1 = f32[16,16]{1,0:T(8,128)} custom-call(f32[10,16,128]{2,1,0:T(8,128)} %get-tuple-element.14.near_part, f32[16,16,128]{2,1,0:T(8,128)} %get-tuple-element.15.far_part, bf16[16,128]{1,0:T(8,128)(2,1)} %get-tuple-element.16.owner), custom_call_target="tpu_custom_call" | custom-call | tf_op jit(solution)/shard_map/home/pallas_call | solution.py:442
  122.6 1.3 %copy.7 = f32[16,16]{1,0:T(8,128)} copy(f32[16,16]{1,0:T(8,128)} %home.1) | data formatting | bytes 2048

commit v2 on v1

--- a/solution.py
+++ b/solution.py
@@ -22,8 +22,8 @@
 ROWS = UROW + 2 * NPROBE
 SUBS = 10
 LANES = 72
-BLOCK = 2
-RLIST = 32
+BLOCK = 4
+RLIST = 40
 FAR = -1.0e30
 SCALE = 1.4426950408889634 / PV
 MESH = pl.DeviceIdType.MESH

time: 124 us -> 105 us (0.85)
  Pallas kernels: 121 us -> 101 us
    pallas_call x1, Pallas kernels: 53.2 us -> 42.6 us  [meet(): pl.pallas_call(meet_kernel, out_shape=(jax.ShapeDtypeStruct((SUBS, NPROBE...]
    pallas_call x1, Pallas kernels: 28.4 us -> 18.9 us  [home(): pl.pallas_call(home_kernel, out_shape=jax.ShapeDtypeStruct((IMGS, NPROBE)...]
where the time goes in v2:
time: 105 us; the launch traced here: 104 us
  Pallas kernels  101 us (96%)
  local copies, waits for them, and re-layouts  3.09 us (3%)
    pallas_call x1, Pallas kernels, meet(): pl.pallas_call(meet_kernel, out_shape=(jax.ShapeDtypeStruct((SUBS, NPROBE...  42.6 us
    pallas_call x1, Pallas kernels, gather(): pl.pallas_call(gather_kernel, out_shape=(jax.ShapeDtypeStruct((GROUPS, RO...  36.9 us
    pallas_call x1, Pallas kernels, home(): pl.pallas_call(home_kernel, out_shape=jax.ShapeDtypeStruct((IMGS, NPROBE)...  18.9 us
    pallas_call x1, Pallas kernels, pack(): pl.pallas_call(pack_kernel, out_shape=(jax.ShapeDtypeStruct((ROWS, 128),...  2.29 us

profile of v2, /device:TPU:1, one launch (start us, length us, event | category | flops | bytes accessed | tf_op | source)
XLA Modules:
  0.0 103.9 jit_solution(6898135438222658088)
XLA Ops:
  0.0 1.8 %reshape.3.x_ref = bf16[784,75]{1,0:T(8,128)(2,1)} reshape(bf16[16,3675]{1,0:T(8,128)(2,1)} %param.5) | data formatting | bytes 235200 | tf_op jit(solution)/shard_map/reshape | solution.py:461
  1.8 2.3 %pack.1 = (bf16[592,128]{1,0:T(8,128)(2,1)}, bf16[16,128]{1,0:T(8,128)(2,1)}) custom-call(s32[16]{0:T(128)} %counts.1, f32[49]{0:T(128)} %weights.1, bf16[784,75]{1,0:T(8,128)(2,1)} %reshape.3.x_ref, f32[16,16]{1,0:T(8,128)} %probes_ref.1), custom_call_target="tpu_custom_call" | custom-call | tf_op jit(solution)/shard_map/pack/pallas_call | solution.py:92
  4.1 36.9 %gather.1 = (bf16[16,592,128]{2,1,0:T(8,128)(2,1)}, bf16[9,592,128]{2,1,0:T(8,128)(2,1)}) custom-call(bf16[592,128]{1,0:T(8,128)(2,1)} %get-tuple-element.11.item), custom_call_target="tpu_custom_call" | custom-call | tf_op jit(solution)/shard_map/gather/pallas_call | solution.py:203
  41.0 42.6 %meet.1 = (f32[10,16,128]{2,1,0:T(8,128)}, f32[16,16,128]{2,1,0:T(8,128)}) custom-call(s32[4,16]{1,0:T(4,128)} %plan.1, bf16[592,128]{1,0:T(8,128)(2,1)} %get-tuple-element.11.item, bf16[9,592,128]{2,1,0:T(8,128)(2,1)} %get-tuple-element.12.near, bf16[16,592,128]{2,1,0:T(8,128)(2,1)} %get-tuple-element.13.far), custom_call_target="tpu_custom_call" | custom-call | tf_op jit(solution)/shard_map/meet/pallas_call | solution.py:367
  83.7 18.9 %home.1 = f32[16,16]{1,0:T(8,128)} custom-call(f32[10,16,128]{2,1,0:T(8,128)} %get-tuple-element.14.near_part, f32[16,16,128]{2,1,0:T(8,128)} %get-tuple-element.15.far_part, bf16[16,128]{1,0:T(8,128)(2,1)} %get-tuple-element.16.owner), custom_call_target="tpu_custom_call" | custom-call | tf_op jit(solution)/shard_map/home/pallas_call | solution.py:442
  102.6 1.3 %copy.7 = f32[16,16]{1,0:T(8,128)} copy(f32[16,16]{1,0:T(8,128)} %home.1) | data formatting | bytes 2048
